TPU v7x, 32 devices: a whole 2x2x4 slice. The times are simulated.
32 devices in a mesh: groups: 2 (over x), gx: 16 (over z, y, core).
Axes of the slice: x: 2, y: 2, z: 4, core: 2. Of those that a mesh axis runs over, the one named last changes fastest.
Arguments:
- snapshots: bfloat16 [256, 4, 512, 128], P('gx', None, 'groups'), parts along dimension 2, may hold values from -20 to 20
- cell_weights: float32 [512, 128], P(('groups', 'gx')), parts along dimension 0, may hold values from 0.5 to 4.5
- diffusivity: float32 [4, 512, 128], P(None, ('groups', 'gx')), parts along dimension 1, may hold values from 0.2 to 2
Outputs:
- diffused_modes: bfloat16 [256, 4, 512, 128], P(None, None, ('groups', 'gx')), parts along dimension 2
- reduced_operator: float32 [512, 256], P('groups'), parts along dimension 0
There are 2 independent parts, one for each index of `groups`. A program takes and returns all parts, laid end to end along the dimension named above; each array names one. Nothing has to cross between parts.
All inputs are finite; a program needn't handle non-finite values.
Results may differ from a plain program's by a relative error of at most 0.0005.
Values may be sent and summed in bfloat16 or wider, within the bound.
A program may use at most 128 MiB of HBM per device.

v0:
```python
import jax
import jax.numpy as jnp
from jax import lax
from jax.sharding import PartitionSpec as P


def extended(block, sides, width):
    for axis, dim in sides:
        count = lax.axis_size(axis)
        forward = [(i, i + 1) for i in range(count - 1)]
        backward = [(target, source) for source, target in forward]
        low = lax.ppermute(
            lax.slice_in_dim(block, block.shape[dim] - width, None, axis=dim), axis, forward
        )
        high = lax.ppermute(lax.slice_in_dim(block, 0, width, axis=dim), axis, backward)
        block = jnp.concatenate([low, block, high], axis=dim)
    return block


def stencil_apply(padded_x, diffusivity):
    field = padded_x[:, :, 2:-2]
    along_x = (
        -padded_x[:, :, :-4]
        + 16.0 * padded_x[:, :, 1:-3]
        - 30.0 * field
        + 16.0 * padded_x[:, :, 3:-1]
        - padded_x[:, :, 4:]
    ) / 12.0
    padded_y = jnp.pad(field, ((0, 0), (0, 0), (0, 0), (2, 2)))
    along_y = (
        -padded_y[..., :-4]
        + 16.0 * padded_y[..., 1:-3]
        - 30.0 * field
        + 16.0 * padded_y[..., 3:-1]
        - padded_y[..., 4:]
    ) / 12.0
    return diffusivity * (along_x + along_y)


def make_rotation(gram_total):
    lower_factor = jnp.linalg.cholesky(gram_total)
    identity = jnp.eye(gram_total.shape[0], dtype=jnp.float32)
    return jax.scipy.linalg.solve_triangular(lower_factor, identity, lower=True)


def on_device(snapshots, cell_weights, diffusivity):
    highest = lax.Precision.HIGHEST
    pod_block = lax.all_to_all(snapshots, "gx", split_axis=2, concat_axis=0, tiled=True)
    snap_float = pod_block.astype(jnp.float32)
    gram_part = jnp.einsum(
        "svxy,tvxy->st", snap_float, snap_float * cell_weights, precision=highest
    )
    cell_count = pod_block.shape[1] * pod_block.shape[2] * pod_block.shape[3] * lax.axis_size("gx")
    padded_raw = extended(pod_block, (("gx", 2),), 2)
    diffused_raw = stencil_apply(padded_raw.astype(jnp.float32), diffusivity)
    cross_part = jnp.einsum(
        "svxy,tvxy->st", snap_float * cell_weights, diffused_raw, precision=highest
    )
    gram_sum_all, cross_sum_all = lax.psum((gram_part, cross_part), "gx")
    rotation = make_rotation(gram_sum_all / cell_count)
    cross_total = cross_sum_all / cell_count
    reduced = jnp.dot(
        jnp.dot(rotation, cross_total, precision=highest), rotation.T, precision=highest
    )
    diffused = jnp.einsum("st,tvxy->svxy", rotation, diffused_raw, precision=highest)
    return (diffused.astype(jnp.bfloat16), reduced)


def solution(mesh):
    in_specs = (
        P("gx", None, "groups", None),
        P(("groups", "gx"), None),
        P(None, ("groups", "gx"), None),
    )
    out_specs = (P(None, None, ("groups", "gx"), None), P("groups", None))
    return jax.shard_map(
        on_device, mesh=mesh, in_specs=in_specs, out_specs=out_specs, check_vma=False
    )
```

profile of v0, /device:TPU:0, one launch (start us, length us, event | category | flops | bytes accessed | tf_op | source)
XLA Modules:
  0.0 352.7 jit_solution(6415887800945460660)
XLA Ops:
  7.2 0.0 copy-start.3
  7.2 6.9 %copy.12 = bf16[16,4,256,128]{3,0,1,2:T(8,128)(2,1)} copy(bf16[16,4,256,128]{3,2,1,0:T(8,128)(2,1)} %param.3) | data formatting | bytes 8388608 | tf_op args[0]
  14.1 7.6 %all-to-all-start = ((bf16[16,4,256,128]{3,0,1,2:T(8,128)(2,1)}), bf16[16,4,256,128]{3,0,1,2:T(8,128)(2,1)}, u32[]{:S(2)}, u32[]{:S(2)}) async-start(bf16[16,4,256,128]{3,0,1,2:T(8,128)(2,1)} %copy.12), calls=%async_computation | async-start | bytes 8388608 | tf_op jit(solution)/shard_map/all_to_all | solution.py:48
  21.7 0.0 all-reduce.5.cloned.1.call-start
  21.7 0.0 copy-done.3
  21.8 77.5 %all-to-all-done = bf16[16,4,256,128]{3,0,1,2:T(8,128)(2,1)} async-done(((bf16[16,4,256,128]{3,0,1,2:T(8,128)(2,1)}), bf16[16,4,256,128]{3,0,1,2:T(8,128)(2,1)}, u32[]{:S(2)}, u32[]{:S(2)}) %all-to-all-start) | async-done | bytes 4194336 | tf_op jit(solution)/shard_map/all_to_all | solution.py:48
  99.2 3.4 copy.13
  102.6 0.0 copy-start
  102.6 0.1 fusion.37
  102.7 2.9 collective-permute-start
  105.7 1.8 collective-permute-start.1
  107.4 0.0 copy-done.2
  107.4 3.3 convert_multiply_fusion
  110.7 4.5 %convolution_bitcast_fusion = f32[256,256]{0,1:T(8,128)} fusion(f32[256,4,16,128]{3,0,2,1:T(8,128)S(1)} %bitcast.59, bf16[256,4,16,128]{3,0,2,1:T(8,128)(2,1)S(1)} %bitcast.56), kind=kOutput, calls=%fused_computation.30 | convolution fusion | flops 6442450944 | bytes 12845056 | tf_op jit(solution)/shard_map/svxy,tvxy->st/dot_general | solution.py:50
  115.2 0.0 copy-done
  115.2 0.0 collective-permute-done
  115.2 0.0 collective-permute-done.1
  115.2 2.7 maximum_convert_fusion
  117.9 3.8 %slice.107 = f32[256,4,16,128]{3,0,2,1:T(8,128)} slice(f32[256,4,20,128]{3,0,2,1:T(8,128)S(1)} %maximum_convert_fusion), slice={[0:256], [0:4], [2:18], [0:128]} | slice | bytes 16777216 | tf_op jit(solution)/shard_map/slice | solution.py:21
  121.7 24.1 %fusion.6 = f32[256,4,16,128]{3,0,2,1:T(8,128)} fusion(f32[256,4,16,128]{3,0,2,1:T(8,128)} %slice.107, f32[256,4,20,128]{3,0,2,1:T(8,128)S(1)} %maximum_convert_fusion, f32[4,16,128]{2,1,0:T(8,128)S(1)} %broadcast_multiply_fusion.1), kind=kLoop, calls=%fused_computation.12 | loop fusion | flops 35651584 | bytes 50364416 | tf_op jit(solution)/shard_map/mul | solution.py:37
  145.8 11.2 %fusion.16 = f32[256,256]{0,1:T(8,128)} fusion(f32[256,4,16,128]{3,0,2,1:T(8,128)} %fusion.6, bf16[256,4,16,128]{3,0,2,1:T(8,128)(2,1)} %bitcast.58, f32[16,128]{1,0:T(8,128)S(1)} %copy-done.2), kind=kOutput, calls=%fused_computation.29 | convolution fusion | flops 6446645248 | bytes 12853248 | tf_op jit(solution)/shard_map/svxy,tvxy->st/dot_general | solution.py:56
  157.0 0.0 all-reduce.5.cloned.1.call-update
  157.1 109.4 %all-reduce.5.cloned.1.call-done = (f32[256,256]{0,1:T(8,128)}, f32[256,256]{0,1:T(8,128)}) async-done(((f32[256,256]{0,1:T(8,128)}, f32[256,256]{0,1:T(8,128)}), (f32[256,256]{0,1:T(8,128)}, f32[256,256]{0,1:T(8,128)})) %all-reduce.5.cloned.1.call-update) | async-done | bytes 524304 | tf_op jit(solution)/shard_map/psum | solution.py:59
  266.5 1.0 broadcast_multiply_fusion
  267.5 0.1 copy.14
  267.6 1.0 fusion.20
  268.6 11.7 %cholesky.50 = f32[128,128]{1,0:T(8,128)S(1)} custom-call(f32[128,128]{1,0:T(8,128)S(1)} %cholesky.118), custom_call_target="Cholesky" | custom-call | tf_op jit(solution)/shard_map/jit(cholesky)/cholesky | solution.py:41
  280.3 9.8 %custom-call.15 = f32[1,128,128]{1,2,0:T(8,128)S(1)} custom-call(f32[1,128,128]{2,1,0:T(8,128)S(1)} %get-tuple-element.33), custom_call_target="InvertDiagBlocksLowerTriangular" | custom-call | tf_op jit(solution)/shard_map/jit(cholesky)/cholesky | solution.py:41
  290.2 0.2 constant_dynamic-update-slice_fusion.1
  290.4 0.3 convolution_subtract_fusion.1
  290.7 11.7 %cholesky.105 = f32[128,128]{1,0:T(8,128)S(1)} custom-call(f32[128,128]{1,0:T(8,128)S(1)} %convolution_subtract_fusion.1), custom_call_target="Cholesky" | custom-call | tf_op jit(solution)/shard_map/jit(cholesky)/cholesky | solution.py:41
  302.4 0.7 compare_reduce_fusion
  304.5 0.1 triangular_solve.63
  304.6 4.1 %while.1 = (s32[]{:T(128)}, f32[256,256]{1,0:T(8,128)S(1)}, s32[2,2]{1,0:T(2,128)S(1)}, f32[2,128,128]{2,1,0:T(8,128)S(1)}, s32[]{:T(128)}) while((s32[]{:T(128)}, f32[256,256]{1,0:T(8,128)S(1)}, s32[2,2]{1,0:T(2,128)S(1)}, f32[2,128,128]{2,1,0:T(8,128)S(1)}, s32[]{:T(128)}) %tuple.31), condition=%wide.while_cond, body=%wide.while_body.sunk | while | flops 2 | bytes 131189 | solution.py:43
  304.6 0.6 fusion.48
  305.2 1.4 bitcast_dynamic-update-slice_fusion.2
  306.6 0.6 fusion.48
  307.2 1.4 bitcast_dynamic-update-slice_fusion.2
  308.6 19.9 %custom-call.16 = f32[2,128,128]{1,2,0:T(8,128)S(1)} custom-call(f32[2,128,128]{2,1,0:T(8,128)S(1)} %get-tuple-element.9), custom_call_target="InvertDiagBlocksLowerTriangular" | custom-call | tf_op jit(solution)/shard_map/jit(_solve_triangular)/triangular_solve | solution.py:43
  328.5 0.3 fusion.25
  328.8 0.3 convolution_subtract_fusion
  329.1 0.3 fusion.28
  329.4 0.0 copy-start.1
  329.4 10.0 %convolution_convert_fusion = bf16[256,4,16,128]{3,0,2,1:T(8,128)(2,1)S(1)} fusion(f32[256,4,16,128]{3,0,2,1:T(8,128)} %fusion.6, f32[128,256]{1,0:T(8,128)S(1)} %fusion.28, f32[128,256]{1,0:T(8,128)S(1)} %fusion.25), kind=kOutput, calls=%fused_computation.28 | convolution fusion | flops 6444613632 | bytes 12845056 | tf_op jit(solution)/shard_map/st,tvxy->svxy/dot_general | solution.py:65
  339.4 4.7 %copy.16 = bf16[256,4,16,128]{3,2,1,0:T(8,128)(2,1)} copy(bf16[256,4,16,128]{3,0,2,1:T(8,128)(2,1)S(1)} %convolution_convert_fusion) | data formatting | bytes 8388608
  344.1 0.0 copy-done.1
  344.1 0.4 fusion.21
  344.6 1.1 fusion.23
  (12 shorter events, 0.2 us)
Async XLA Ops:
  7.2 14.6 %copy-start.3 = (f32[4,16,128]{2,1,0:T(8,128)S(1)}, f32[4,16,128]{2,1,0:T(8,128)}, u32[]{:S(2)}) copy-start(f32[4,16,128]{2,1,0:T(8,128)} %param.5) | copy-start | bytes 98308
  14.1 93.3 %copy-start.2 = (f32[16,128]{1,0:T(8,128)S(1)}, f32[16,128]{1,0:T(8,128)}, u32[]{:S(2)}) copy-start(f32[16,128]{1,0:T(8,128)} %param.4) | copy-start | bytes 24580
  14.1 85.1 %all-to-all-start = ((bf16[16,4,256,128]{3,0,1,2:T(8,128)(2,1)}), bf16[16,4,256,128]{3,0,1,2:T(8,128)(2,1)}, u32[]{:S(2)}, u32[]{:S(2)}) async-start(bf16[16,4,256,128]{3,0,1,2:T(8,128)(2,1)} %copy.12), calls=%async_computation | async-start | bytes 8388608 | tf_op jit(solution)/shard_map/all_to_all | solution.py:48
  21.7 244.8 %all-reduce.5.cloned.1.call-start = ((), (), s32[]{:S(2)}) async-start(), calls=%async_computation.1 | async-start | bytes 1048576 | tf_op jit(solution)/shard_map/psum | solution.py:59
  102.6 12.6 %copy-start = (bf16[16,4,16,16,128]{4,0,2,3,1:T(8,128)(2,1)}, bf16[16,4,16,16,128]{4,0,2,3,1:T(8,128)(2,1)S(1)}, u32[]{:S(2)}) copy-start(bf16[16,4,16,16,128]{4,0,2,3,1:T(8,128)(2,1)S(1)} %copy.13) | copy-start | bytes 12582916
  102.7 12.5 %collective-permute-start = (bf16[256,4,2,128]{3,0,2,1:T(8,128)(2,1)S(1)}, bf16[256,4,2,128]{3,0,2,1:T(8,128)(2,1)S(1)}, u32[]{:S(2)}, u32[]{:S(2)}) collective-permute-start(bf16[256,4,2,128]{3,0,2,1:T(8,128)(2,1)S(1)} %get-tuple-element.28), channel_id=1, source_target_pairs={{0,1},{1,2},{2,3},{3,4},{4,5},{5,6},{6,7},{7,8},{8,9},{9,10},{10,1... | collective-permute-start | bytes 1572872 | tf_op jit(solution)/shard_map/ppermute | solution.py:12
  105.7 9.6 %collective-permute-start.1 = (bf16[256,4,2,128]{3,0,2,1:T(8,128)(2,1)S(1)}, bf16[256,4,2,128]{3,0,2,1:T(8,128)(2,1)S(1)}, u32[]{:S(2)}, u32[]{:S(2)}) collective-permute-start(bf16[256,4,2,128]{3,0,2,1:T(8,128)(2,1)S(1)} %get-tuple-element.29), channel_id=1, source_target_pairs={{1,0},{2,1},{3,2},{4,3},{5,4},{6,5},{7,6},{8,7},{9,8},{10,9},{11,1... | collective-permute-start | bytes 1572872 | tf_op jit(solution)/shard_map/ppermute | solution.py:15
  329.4 14.8 %copy-start.1 = (f32[256,256]{0,1:T(8,128)S(1)}, f32[256,256]{0,1:T(8,128)}, u32[]{:S(2)}) copy-start(f32[256,256]{0,1:T(8,128)} %get-tuple-element.25) | copy-start | bytes 786436
Sparse Core Ops, SparseCore 0:
  157.1 109.2 all-reduce.4
where the time goes:
time: 357 us; the launch traced here: 353 us
  waiting for transfers between devices  187 us (52%)
  other arithmetic  86 us (24%)
  matrix products  28.6 us (8%)
  local copies, waits for them, and re-layouts  23.1 us (6%)
  between operations  15.8 us (4%)
  starting transfers between devices  12.3 us (3%)
    psum x1, waiting for transfers between devices, on_device(): gram_sum_all, cross_sum_all = lax.psum((gram_part, cross_part), 'gx')  109 us
    all_to_all x1, waiting for transfers between devices, on_device(): lax.all_to_all(snapshots, 'gx', split_axis=2, concat_axis=0, tiled=True)  77.5 us
    another operation x6, other arithmetic, make_rotation(): lower_factor = jnp.linalg.cholesky(gram_total)  34 us
    mul x2, other arithmetic, stencil_apply(): return diffusivity * (along_x + along_y)  24.1 us
    another operation x3, other arithmetic, make_rotation(): return jax.scipy.linalg.solve_triangular(lower_factor, identity, lower=True)  19.9 us
    unnamed x10, local copies, waits for them, and re-layouts  11.6 us
    dot_general x1, matrix products, on_device(): jnp.einsum('svxy,tvxy->st', snap_float * cell_weights, diffused_raw, prec...  11.2 us
    dot_general x1, matrix products, on_device(): jnp.einsum('st,tvxy->svxy', rotation, diffused_raw, precision=highest)  10 us
  transfers between devices with their start and end apart: 4, of which 2 were waited for; matrix products, arithmetic and copies ran while one was open for 2% of the time, Pallas kernels for 0%

commit v1 on v0

--- a/solution.py
+++ b/solution.py
@@ -45,7 +45,10 @@
 
 def on_device(snapshots, cell_weights, diffusivity):
     highest = lax.Precision.HIGHEST
-    pod_block = lax.all_to_all(snapshots, "gx", split_axis=2, concat_axis=0, tiled=True)
+    pod_block = jnp.concatenate(
+        lax.all_to_all(jnp.stack(jnp.split(snapshots, lax.axis_size("gx"), axis=2)), "gx", 0, 0),
+        axis=0,
+    )
     snap_float = pod_block.astype(jnp.float32)
     gram_part = jnp.einsum(
         "svxy,tvxy->st", snap_float, snap_float * cell_weights, precision=highest

time: 357 us -> 382 us (1.070)
  local copies, waits for them, and re-layouts: 23.1 us -> 44.6 us
  matrix products: 28.6 us -> 33.6 us
    unnamed x10 -> x24, local copies, waits for them, and re-layouts: 11.6 us -> 29.9 us
    dot_general x1, matrix products: 4.48 us -> 9.58 us  [on_device(): jnp.einsum('svxy,tvxy->st', snap_float, snap_float * cell_weights, precis...]
  transfers between devices with their start and end apart: 4 -> 4, of which waited for: 2 -> 2; matrix products, arithmetic and copies ran while one was open for 2% -> 3% of each run, Pallas kernels for 0% -> 0%
where the time goes in v1:
time: 382 us; the launch traced here: 378 us
  waiting for transfers between devices  185 us (48%)
  other arithmetic  86.6 us (23%)
  local copies, waits for them, and re-layouts  44.6 us (12%)
  matrix products  33.6 us (9%)
  between operations  15.8 us (4%)
  starting transfers between devices  12.1 us (3%)
    psum x1, waiting for transfers between devices, on_device(): gram_sum_all, cross_sum_all = lax.psum((gram_part, cross_part), 'gx')  108 us
    all_to_all x1, waiting for transfers between devices, on_device(): lax.all_to_all(jnp.stack(jnp.split(snapshots, lax.axis_size('gx'), axis=2...  77.5 us
    another operation x6, other arithmetic, make_rotation(): lower_factor = jnp.linalg.cholesky(gram_total)  34 us
    unnamed x24, local copies, waits for them, and re-layouts  29.9 us
    mul x2, other arithmetic, stencil_apply(): return diffusivity * (along_x + along_y)  24.1 us
    another operation x3, other arithmetic, make_rotation(): return jax.scipy.linalg.solve_triangular(lower_factor, identity, lower=True)  19.9 us
    dot_general x1, matrix products, on_device(): jnp.einsum('svxy,tvxy->st', snap_float * cell_weights, diffused_raw, prec...  11.2 us
    dot_general x1, matrix products, on_device(): jnp.einsum('st,tvxy->svxy', rotation, diffused_raw, precision=highest)  9.98 us
  transfers between devices with their start and end apart: 4, of which 2 were waited for; matrix products, arithmetic and copies ran while one was open for 3% of the time, Pallas kernels for 0%

profile of v1, /device:TPU:0, one launch (start us, length us, event | category | flops | bytes accessed | tf_op | source)
XLA Modules:
  0.0 378.0 jit_solution(3568269106964519062)
XLA Ops:
  7.2 1.7 bitcast_dynamic-update-slice_fusion.16
  8.8 1.7 bitcast_dynamic-update-slice_fusion.15
  10.5 1.7 bitcast_dynamic-update-slice_fusion.14
  12.2 1.7 bitcast_dynamic-update-slice_fusion.13
  13.9 1.7 bitcast_dynamic-update-slice_fusion.12
  15.6 1.7 bitcast_dynamic-update-slice_fusion.11
  17.2 1.7 bitcast_dynamic-update-slice_fusion.10
  18.9 1.7 bitcast_dynamic-update-slice_fusion.9
  20.6 1.7 bitcast_dynamic-update-slice_fusion.8
  22.3 1.7 bitcast_dynamic-update-slice_fusion.7
  24.0 1.7 bitcast_dynamic-update-slice_fusion.6
  25.6 1.7 bitcast_dynamic-update-slice_fusion.5
  27.3 1.7 bitcast_dynamic-update-slice_fusion.4
  29.0 1.7 bitcast_dynamic-update-slice_fusion.3
  30.7 1.7 bitcast_dynamic-update-slice_fusion.2
  32.4 1.7 bitcast_dynamic-update-slice_fusion.1
  34.0 7.6 %all-to-all-start = ((bf16[16,16,4,16,128]{4,3,2,1,0:T(8,128)(2,1)}), bf16[16,16,4,16,128]{4,3,2,1,0:T(8,128)(2,1)}, u32[]{:S(2)}, u32[]{:S(2)}) async-start(bf16[16,16,4,16,128]{4,3,2,1,0:T(8,128)(2,1)} %bitcast_dynamic-update-slice_fusion.1), calls=%async_computation | async-start | bytes 8388608 | tf_op jit(solution)/shard_map/all_to_all | solution.py:49
  41.7 77.5 %all-to-all-done = bf16[16,16,4,16,128]{4,3,2,1,0:T(8,128)(2,1)} async-done(((bf16[16,16,4,16,128]{4,3,2,1,0:T(8,128)(2,1)}), bf16[16,16,4,16,128]{4,3,2,1,0:T(8,128)(2,1)}, u32[]{:S(2)}, u32[]{:S(2)}) %all-to-all-start) | async-done | bytes 4194336 | tf_op jit(solution)/shard_map/all_to_all | solution.py:49
  119.2 4.9 %copy.5 = bf16[16,16,4,16,128]{4,1,0,3,2:T(8,128)(2,1)S(1)} copy(bf16[16,16,4,16,128]{4,3,2,1,0:T(8,128)(2,1)} %all-to-all-done) | data formatting | bytes 8388608 | tf_op jit(solution)/shard_map/all_to_all | solution.py:49
  124.2 2.9 collective-permute-start
  127.1 1.6 collective-permute-start.1
  128.7 3.4 convert_multiply_fusion
  132.1 9.6 %fusion.21 = f32[256,256]{0,1:T(8,128)} fusion(bf16[256,4,16,128]{3,0,2,1:T(8,128)(2,1)S(1)} %bitcast.81, f32[256,4,16,128]{3,2,1,0:T(8,128)S(1)} %bitcast.84), kind=kOutput, calls=%fused_computation.32 | convolution fusion | flops 6442450944 | bytes 12845056 | tf_op jit(solution)/shard_map/svxy,tvxy->st/dot_general | solution.py:53
  141.7 3.2 maximum_convert_fusion
  144.9 3.8 slice.107
  148.6 24.1 %fusion.6 = f32[256,4,16,128]{3,0,2,1:T(8,128)} fusion(f32[256,4,16,128]{3,0,2,1:T(8,128)} %slice.107, f32[256,4,20,128]{3,0,2,1:T(8,128)S(1)} %maximum_convert_fusion, f32[4,16,128]{2,1,0:T(8,128)S(1)} %broadcast_multiply_fusion.1), kind=kLoop, calls=%fused_computation.12 | loop fusion | flops 35651584 | bytes 50364416 | tf_op jit(solution)/shard_map/mul | solution.py:37
  172.7 11.2 %fusion.18 = f32[256,256]{0,1:T(8,128)} fusion(f32[256,4,16,128]{3,0,2,1:T(8,128)} %fusion.6, bf16[256,4,16,128]{3,0,2,1:T(8,128)(2,1)} %bitcast.83, f32[16,128]{1,0:T(8,128)S(1)} %copy-done.2), kind=kOutput, calls=%fused_computation.31 | convolution fusion | flops 6446645248 | bytes 12853248 | tf_op jit(solution)/shard_map/svxy,tvxy->st/dot_general | solution.py:59
  184.1 107.7 %all-reduce.5.cloned.1.call-done = (f32[256,256]{0,1:T(8,128)}, f32[256,256]{0,1:T(8,128)}) async-done(((f32[256,256]{0,1:T(8,128)}, f32[256,256]{0,1:T(8,128)}), (f32[256,256]{0,1:T(8,128)}, f32[256,256]{0,1:T(8,128)})) %all-reduce.5.cloned.1.call-update) | async-done | bytes 524304 | tf_op jit(solution)/shard_map/psum | solution.py:62
  291.7 1.0 broadcast_multiply_fusion
  292.8 1.0 fusion.25
  293.8 11.7 %cholesky.50 = f32[128,128]{1,0:T(8,128)S(1)} custom-call(f32[128,128]{1,0:T(8,128)S(1)} %cholesky.118), custom_call_target="Cholesky" | custom-call | tf_op jit(solution)/shard_map/jit(cholesky)/cholesky | solution.py:41
  305.6 9.8 %custom-call.15 = f32[1,128,128]{1,2,0:T(8,128)S(1)} custom-call(f32[1,128,128]{2,1,0:T(8,128)S(1)} %get-tuple-element.29), custom_call_target="InvertDiagBlocksLowerTriangular" | custom-call | tf_op jit(solution)/shard_map/jit(cholesky)/cholesky | solution.py:41
  315.6 0.3 convolution_subtract_fusion.1
  315.9 11.7 %cholesky.105 = f32[128,128]{1,0:T(8,128)S(1)} custom-call(f32[128,128]{1,0:T(8,128)S(1)} %convolution_subtract_fusion.1), custom_call_target="Cholesky" | custom-call | tf_op jit(solution)/shard_map/jit(cholesky)/cholesky | solution.py:41
  327.7 0.7 compare_reduce_fusion
  329.8 4.1 %while.1 = (s32[]{:T(128)}, f32[256,256]{1,0:T(8,128)S(1)}, s32[2,2]{1,0:T(2,128)S(1)}, f32[2,128,128]{2,1,0:T(8,128)S(1)}, s32[]{:T(128)}) while((s32[]{:T(128)}, f32[256,256]{1,0:T(8,128)S(1)}, s32[2,2]{1,0:T(2,128)S(1)}, f32[2,128,128]{2,1,0:T(8,128)S(1)}, s32[]{:T(128)}) %tuple.29), condition=%wide.while_cond, body=%wide.while_body.sunk | while | flops 2 | bytes 131189 | solution.py:43
  329.8 0.6 fusion.52
  330.4 1.4 bitcast_dynamic-update-slice_fusion.18
  331.9 0.6 fusion.52
  332.4 1.4 bitcast_dynamic-update-slice_fusion.18
  333.9 19.9 %custom-call.16 = f32[2,128,128]{1,2,0:T(8,128)S(1)} custom-call(f32[2,128,128]{2,1,0:T(8,128)S(1)} %get-tuple-element.9), custom_call_target="InvertDiagBlocksLowerTriangular" | custom-call | tf_op jit(solution)/shard_map/jit(_solve_triangular)/triangular_solve | solution.py:43
  353.8 0.3 fusion.30
  354.0 0.3 convolution_subtract_fusion
  354.3 0.3 fusion.33
  354.6 10.0 %convolution_convert_fusion = bf16[256,4,16,128]{3,0,2,1:T(8,128)(2,1)S(1)} fusion(f32[256,4,16,128]{3,0,2,1:T(8,128)} %fusion.6, f32[128,256]{1,0:T(8,128)S(1)} %fusion.33, f32[128,256]{1,0:T(8,128)S(1)} %fusion.30), kind=kOutput, calls=%fused_computation.30 | convolution fusion | flops 6444613632 | bytes 12845056 | tf_op jit(solution)/shard_map/st,tvxy->svxy/dot_general | solution.py:68
  364.6 4.7 %copy.9 = bf16[256,4,16,128]{3,2,1,0:T(8,128)(2,1)} copy(bf16[256,4,16,128]{3,0,2,1:T(8,128)(2,1)S(1)} %convolution_convert_fusion) | data formatting | bytes 8388608
  369.4 0.4 fusion.26
  369.8 1.1 fusion.28
  (27 shorter events, 0.8 us)
Async XLA Ops:
  34.0 7.7 %copy-start.3 = (f32[4,16,128]{2,1,0:T(8,128)S(1)}, f32[4,16,128]{2,1,0:T(8,128)}, u32[]{:S(2)}) copy-start(f32[4,16,128]{2,1,0:T(8,128)} %param.5) | copy-start | bytes 98308
  34.0 85.1 %all-to-all-start = ((bf16[16,16,4,16,128]{4,3,2,1,0:T(8,128)(2,1)}), bf16[16,16,4,16,128]{4,3,2,1,0:T(8,128)(2,1)}, u32[]{:S(2)}, u32[]{:S(2)}) async-start(bf16[16,16,4,16,128]{4,3,2,1,0:T(8,128)(2,1)} %bitcast_dynamic-update-slice_fusion.1), calls=%async_computation | async-start | bytes 8388608 | tf_op jit(solution)/shard_map/all_to_all | solution.py:49
  41.6 250.1 %all-reduce.5.cloned.1.call-start = ((), (), s32[]{:S(2)}) async-start(), calls=%async_computation.1 | async-start | bytes 1048576 | tf_op jit(solution)/shard_map/psum | solution.py:62
  41.7 87.0 %copy-start.2 = (f32[16,128]{1,0:T(8,128)S(1)}, f32[16,128]{1,0:T(8,128)}, u32[]{:S(2)}) copy-start(f32[16,128]{1,0:T(8,128)} %param.4) | copy-start | bytes 24580
  124.1 8.0 %copy-start = (bf16[16,16,4,16,128]{4,1,0,3,2:T(8,128)(2,1)}, bf16[16,16,4,16,128]{4,1,0,3,2:T(8,128)(2,1)S(1)}, u32[]{:S(2)}) copy-start(bf16[16,16,4,16,128]{4,1,0,3,2:T(8,128)(2,1)S(1)} %copy.5) | copy-start | bytes 12582916
  124.2 17.5 %collective-permute-start = (bf16[256,4,2,128]{3,0,2,1:T(8,128)(2,1)S(1)}, bf16[256,4,2,128]{3,0,2,1:T(8,128)(2,1)S(1)}, u32[]{:S(2)}, u32[]{:S(2)}) collective-permute-start(bf16[256,4,2,128]{3,0,2,1:T(8,128)(2,1)S(1)} %get-tuple-element.24), channel_id=1, source_target_pairs={{0,1},{1,2},{2,3},{3,4},{4,5},{5,6},{6,7},{7,8},{8,9},{9,10},{10,1... | collective-permute-start | bytes 1572872 | tf_op jit(solution)/shard_map/ppermute | solution.py:12
  127.1 14.6 %collective-permute-start.1 = (bf16[256,4,2,128]{3,0,2,1:T(8,128)(2,1)S(1)}, bf16[256,4,2,128]{3,0,2,1:T(8,128)(2,1)S(1)}, u32[]{:S(2)}, u32[]{:S(2)}) collective-permute-start(bf16[256,4,2,128]{3,0,2,1:T(8,128)(2,1)S(1)} %get-tuple-element.25), channel_id=1, source_target_pairs={{1,0},{2,1},{3,2},{4,3},{5,4},{6,5},{7,6},{8,7},{9,8},{10,9},{11,1... | collective-permute-start | bytes 1572872 | tf_op jit(solution)/shard_map/ppermute | solution.py:15
  364.6 4.7 %copy-start.1 = (f32[256,256]{0,1:T(8,128)S(1)}, f32[256,256]{0,1:T(8,128)}, u32[]{:S(2)}) copy-start(f32[256,256]{0,1:T(8,128)} %get-tuple-element.21) | copy-start | bytes 786436
Sparse Core Ops, SparseCore 0:
  184.1 107.5 all-reduce.4
